TPU v7x, 256 devices: a whole 4x4x8 slice. The times are simulated.
256 devices in a mesh: dst: 32 (over y, z), src: 8 (over x, core).
Axes of the slice: x: 4, y: 4, z: 8, core: 2. Of those that a mesh axis runs over, the one named last changes fastest.
Arguments:
- features: bfloat16 [131072, 128], P(('src', 'dst')), may hold values from -64 to 64
- projection: bfloat16 [128, 256], replicated, may hold values from -1 to 1
- source_att: float32 [256], replicated, may hold values from -1.5 to 1.5
- target_att: float32 [256], replicated, may hold values from -1 to 1
- out_bias: float32 [256], replicated, may hold values from -3 to 3
- block_coords: int32 [32, 8, 2, 256], P('dst', 'src'), may hold values from 0 to 127, as said below
- block_words: int32 [32, 8, 256, 16, 128], P('dst', 'src'), may hold values from 0 to 255, as said below
- block_counts: int32 [32, 8], P('dst', 'src'), may hold values from 1 to 256, as said below
Outputs:
- result: bfloat16 [131072, 256], P(('dst', 'src'))
Inputs may be any that keep to these rules, and one draw needn't show every extreme that they name: `block_coords`: row entries are below 32 and column entries below 128; the (row, column) pairs of one device's slots are distinct. `block_counts`: at least one device has all 256 slots live. `block_words`: each word holds an 8-bit pattern.
All inputs are finite; a program needn't handle non-finite values.
Results may differ from a plain program's by a relative error of at most 0.019.
Values may be sent and summed in bfloat16 or wider, within the bound.
No kernel may reach another device: no remote copies, remote signals or barrier semaphores. Data moves between devices by JAX's collectives and lax.ppermute only.
A program may use at most 128 MiB of HBM per device.

v0:
```python
import math
import jax
import jax.numpy as jnp
from jax import lax
from jax.sharding import PartitionSpec as P

HEADS = 8
HEAD_DIM = 32


def from_root(block, axis, holder):
    block = jnp.where(lax.axis_index(axis) == holder, block, jnp.zeros_like(block))
    return lax.psum(block, axis)


def leaky_relu(inputs):
    return jnp.where(inputs > 0, inputs, 0.2 * inputs)


def unpack(packed):
    shifts = jnp.arange(8, dtype=jnp.int32)
    spread = jnp.right_shift(packed[..., :, None, :], shifts[:, None]) & 1
    leading = packed.shape[:-2]
    flattened = spread.reshape(leading + (128, 128))
    return jnp.swapaxes(flattened, -1, -2) > 0


def terms_of(projected, source_att, target_att):
    source_part = jnp.sum(
        (projected * source_att).reshape(projected.shape[0], HEADS, HEAD_DIM), axis=-1
    )
    target_part = jnp.sum(
        (projected * target_att).reshape(projected.shape[0], HEADS, HEAD_DIM), axis=-1
    )
    return jnp.concatenate([source_part, target_part], axis=1).T


def on_device(
    features, projection, source_att, target_att, out_bias, block_coords, block_words, block_counts
):
    dst_count = lax.axis_size("dst")
    src_count = lax.axis_size("src")
    group_ratio = dst_count // src_count
    dst_index = lax.axis_index("dst")
    src_index = lax.axis_index("src")
    root_index = dst_index // group_ratio
    own_rows = features.shape[0]
    rows_dst = own_rows * src_count
    feature_width = projection.shape[1]
    projected = jnp.dot(features, projection, preferred_element_type=jnp.float32)
    gathered, score_terms = (
        lax.all_gather(projected.astype(jnp.bfloat16), "dst", axis=0, tiled=True),
        lax.all_gather(
            terms_of(projected, source_att, target_att).astype(jnp.bfloat16),
            "dst",
            axis=1,
            tiled=True,
        ).astype(jnp.float32),
    )
    src_rows = gathered.shape[0]
    row_blocks = rows_dst // 128
    col_blocks = src_rows // 128
    offset = dst_index % group_ratio * rows_dst
    target_own = lax.dynamic_slice_in_dim(score_terms[HEADS:], offset, rows_dst, 1)
    target_rows = from_root(target_own.astype(jnp.bfloat16), "src", root_index).astype(
        target_own.dtype
    )
    target_blocks = target_rows.reshape(HEADS, row_blocks, 128).transpose(1, 0, 2)
    source_blocks = score_terms[:HEADS].reshape(HEADS, col_blocks, 128).transpose(1, 0, 2)
    value_blocks = gathered.reshape(col_blocks, 128, HEADS, HEAD_DIM)
    self_source = (
        lax.dynamic_slice_in_dim(score_terms[:HEADS], offset, rows_dst, 1)
        .reshape(HEADS, row_blocks, 128)
        .transpose(1, 0, 2)
    )
    self_score = leaky_relu(target_blocks + self_source)
    is_root = src_index == root_index
    coords = block_coords[0, 0]
    packed_words = block_words[0, 0]
    live_count = block_counts[0, 0]
    group_size = math.gcd(packed_words.shape[0], 16)
    steps_live = (live_count + group_size - 1) // group_size

    def group_scores(step_index):
        first_slot = step_index * group_size
        row_ids = lax.dynamic_slice_in_dim(coords[0], first_slot, group_size)
        col_ids = lax.dynamic_slice_in_dim(coords[1], first_slot, group_size)
        packed = lax.dynamic_slice_in_dim(packed_words, first_slot, group_size, 0)
        valid_slot = first_slot + jnp.arange(group_size, dtype=jnp.int32) < live_count
        edge_mask = unpack(packed) & valid_slot[:, None, None]
        scores = leaky_relu(
            target_blocks[row_ids][:, :, :, None] + source_blocks[col_ids][:, :, None, :]
        )
        return (row_ids, col_ids, edge_mask, scores)

    def max_step(step_index, maxima):
        row_ids, col_ids, edge_mask, scores = group_scores(step_index)
        block_max = jnp.max(jnp.where(edge_mask[:, None], scores, -jnp.inf), axis=3)
        return maxima.at[row_ids].max(block_max)

    maxima = lax.fori_loop(
        0, steps_live, max_step, jnp.full((row_blocks, HEADS, 128), -jnp.inf, jnp.float32)
    )
    maxima = jnp.where(is_root, jnp.maximum(maxima, self_score), maxima)
    maxima = lax.pmax(maxima.astype(jnp.bfloat16), "src").astype(maxima.dtype)

    def sum_step(step_index, carry_state):
        weighted, denominator = carry_state
        row_ids, col_ids, edge_mask, scores = group_scores(step_index)
        weight = jnp.where(edge_mask[:, None], jnp.exp(scores - maxima[row_ids][..., None]), 0.0)
        rounded = weight.astype(jnp.bfloat16)
        contrib = jnp.einsum(
            "ghab,gbhc->gahc", rounded, value_blocks[col_ids], preferred_element_type=jnp.float32
        )
        contrib = contrib.reshape(group_size, 128, feature_width)
        weighted = weighted.at[row_ids].add(contrib)
        denominator = denominator.at[row_ids].add(jnp.sum(weight, axis=3))
        return (weighted, denominator)

    start_state = (
        jnp.zeros((row_blocks, 128, feature_width), jnp.float32),
        jnp.zeros((row_blocks, HEADS, 128), jnp.float32),
    )
    weighted, denominator = lax.fori_loop(0, steps_live, sum_step, start_state)
    self_weight = jnp.where(is_root, jnp.exp(self_score - maxima), 0.0)
    denominator = denominator + self_weight
    self_values = lax.dynamic_slice_in_dim(gathered, offset, rows_dst, 0).reshape(
        row_blocks, 128, HEADS, HEAD_DIM
    )
    self_rounded = lax.optimization_barrier(self_weight.astype(jnp.bfloat16))
    self_part = self_rounded.astype(jnp.float32).transpose(0, 2, 1)[..., None] * self_values.astype(
        jnp.float32
    )
    weighted = weighted + self_part.reshape(row_blocks, 128, feature_width)
    weighted_rows = weighted.reshape(rows_dst, feature_width)
    denominator_rows = denominator.transpose(1, 0, 2).reshape(HEADS, rows_dst)
    weighted_own, denominator_own = (
        lax.psum_scatter(
            weighted_rows.astype(jnp.bfloat16), "src", scatter_dimension=0, tiled=True
        ).astype(jnp.float32),
        lax.psum_scatter(
            denominator_rows.astype(jnp.bfloat16), "src", scatter_dimension=1, tiled=True
        ).astype(jnp.float32),
    )
    mixed_rows = weighted_own.reshape(own_rows, HEADS, HEAD_DIM) / denominator_own.T[:, :, None]
    result = jax.nn.elu(mixed_rows.reshape(own_rows, feature_width) + out_bias)
    return result.astype(jnp.bfloat16)


def solution(mesh):
    placed = (
        P(("src", "dst"), None),
        P(),
        P(),
        P(),
        P(),
        P("dst", "src", None, None),
        P("dst", "src", None, None, None),
        P("dst", "src"),
    )
    return jax.shard_map(
        on_device, mesh=mesh, in_specs=placed, out_specs=P(("dst", "src"), None), check_vma=False
    )
```

profile of v0, /device:TPU:8, one launch (start us, length us, event | category | flops | bytes accessed | tf_op | source)
XLA Modules:
  0.0 1036.6 jit_solution(7176538615227413374)
XLA Ops:
  8.3 1.9 bitcast_reduce_fusion.1
  10.2 52.3 %all_gather.7 = bf16[16,16384]{1,0:T(8,128)(2,1)S(1)} all-gather(bf16[16,512]{1,0:T(8,128)(2,1)S(1)} %maximum_bitcast_fusion), channel_id=1, replica_groups=mesh['dst'=32,'src'=8] {'dst'}, dimensions={1}, use_global_device_ids=true | all-gather | bytes 540672 | tf_op jit(solution)/shard_map/all_gather | solution.py:53
  64.1 61.0 %all-reduce.3.cloned.1.call-done = bf16[32,8,128]{2,1,0:T(8,128)(2,1)} async-done(((bf16[32,8,128]{2,1,0:T(8,128)(2,1)}), bf16[32,8,128]{2,1,0:T(8,128)(2,1)}) %all-reduce.3.cloned.1.call-update) | async-done | bytes 65552 | tf_op jit(solution)/shard_map/psum | solution.py:13
  125.9 38.4 %while.22 = (s32[]{:T(128)}, f32[32,8,128]{2,1,0:T(8,128)S(1)}, s32[]{:T(128)}, s32[2,256]{1,0:T(2,128)S(1)}, s32[256,16,128]{2,1,0:T(8,128)}, /*index=5*/s32[]{...) while((s32[]{:T(128)}, f32[32,8,128]{2,1,0:T(8,128)S(1)}, ...), condition=%wide.region_6.7_spmd, body=%wide.region_3.6_spmd.sunk | while | flops 13633670 | bytes 2112275 | solution.py:101
  129.7 4.7 fusion.61
  139.3 4.7 fusion.61
  148.9 4.7 fusion.61
  153.6 1.1 scatter_fusion
  158.5 4.7 fusion.61
  165.7 175.4 %all-reduce.5.cloned.1.call-done = bf16[32,8,128]{2,1,0:T(8,128)(2,1)} async-done(((bf16[32,8,128]{2,1,0:T(8,128)(2,1)}), bf16[32,8,128]{2,1,0:T(8,128)(2,1)}) %all-reduce.5.cloned.1.call-update) | async-done | bytes 65552 | tf_op jit(solution)/shard_map/pmax | solution.py:105
  341.1 1.5 convert_element_type.61
  342.6 38.5 %all-gather.2.cloned.1.call-done = bf16[16384,256]{0,1:T(8,128)(2,1)} async-done(((bf16[512,256]{0,1:T(8,128)(2,1)}), bf16[16384,256]{0,1:T(8,128)(2,1)}) %all-gather.2.cloned.1.call-update) | async-done | bytes 8388624 | tf_op jit(solution)/shard_map/all_gather | solution.py:52
  381.1 9.2 copy.53
  390.2 24.4 %copy.47 = bf16[128,128,8,32]{3,2,1,0:T(8,128)(2,1)} copy(bf16[128,128,8,32]{1,0,3,2:T(8,128)(2,1)} %bitcast.136) | data formatting | bytes 16777216 | tf_op jit(solution)/shard_map/while | solution.py:124
  414.6 2.4 broadcast_in_dim.36
  417.0 134.6 %while.23 = (s32[]{:T(128)}, f32[32,128,256]{2,1,0:T(8,128)}, f32[32,8,128]{2,1,0:T(8,128)S(1)}, s32[]{:T(128)}, s32[2,256]{1,0:T(2,128)S(1)}, /*index=5*/bf16[1...) while((s32[]{:T(128)}, f32[32,128,256]{2,1,0:T(8,128)}, ...), condition=%wide.region_12.13_spmd, body=%wide.region_8.12_spmd.sunk | while | flops 165152896 | bytes 18496492 | solution.py:124
  417.3 1.5 gather_fusion.3
  419.9 4.9 gather_fusion.2
  427.3 8.3 fusion.67
  435.6 1.9 copy.64
  437.5 4.5 scatter_fusion.1
  442.0 7.6 fusion.68
  450.9 1.5 gather_fusion.3
  453.5 5.0 gather_fusion.2
  461.0 8.3 fusion.67
  469.2 1.9 copy.64
  471.2 4.6 scatter_fusion.1
  475.7 7.6 fusion.68
  484.6 1.5 gather_fusion.3
  487.2 4.9 gather_fusion.2
  494.6 8.3 fusion.67
  502.9 1.9 copy.64
  504.8 4.4 scatter_fusion.1
  509.3 7.6 fusion.68
  516.9 1.1 scatter_fusion.2
  518.1 1.5 gather_fusion.3
  520.8 4.9 gather_fusion.2
  528.1 8.3 fusion.67
  536.4 1.9 copy.64
  538.3 4.5 scatter_fusion.1
  542.9 7.6 fusion.68
  551.6 5.6 copy.49
  557.2 1.6 fusion.42
  558.9 3.6 fusion.35
  562.6 2.9 copy.50
  565.5 424.4 %reduce-scatter.5.cloned.1.call-done = bf16[8,512]{1,0:T(8,128)(2,1)} async-done(((bf16[8,4096]{1,0:T(8,128)(2,1)}), bf16[8,512]{1,0:T(8,128)(2,1)}) %reduce-scatter.5.cloned.1.call-update) | async-done | bytes 8208 | tf_op jit(solution)/shard_map/reduce_scatter | solution.py:141
  990.9 36.6 %reduce-scatter.3.cloned.1.call-done = bf16[512,256]{1,0:T(8,128)(2,1)} async-done(((bf16[4096,256]{1,0:T(8,128)(2,1)}), bf16[512,256]{1,0:T(8,128)(2,1)}) %reduce-scatter.3.cloned.1.call-update) | async-done | bytes 262160 | tf_op jit(solution)/shard_map/reduce_scatter | solution.py:138
  1027.5 1.9 fusion.37
  (140 shorter events, 40.9 us)
Async XLA Ops:
  7.4 0.9 copy-start
  7.4 118.6 %copy-start.5 = (s32[1,1,2,256]{3,2,1,0:T(2,128)S(1)}, s32[1,1,2,256]{3,2,1,0:T(2,128)}, u32[]{:S(2)}) copy-start(s32[1,1,2,256]{3,2,1,0:T(2,128)} %param.17) | copy-start | bytes 6148
  7.4 117.7 %all-reduce.3.cloned.1.call-start = ((), (), s32[]{:S(2)}) async-start(), calls=%async_computation.3 | async-start | bytes 131072 | tf_op jit(solution)/shard_map/psum | solution.py:13
  63.2 277.9 %all-reduce.5.cloned.1.call-start = ((), (), s32[]{:S(2)}) async-start(), calls=%async_computation.4 | async-start | bytes 131072 | tf_op jit(solution)/shard_map/pmax | solution.py:105
  64.1 100.3 %copy-start.2 = (f32[8,16384]{1,0:T(8,128)}, f32[8,16384]{1,0:T(8,128)S(1)}, u32[]{:S(2)}) copy-start(f32[8,16384]{1,0:T(8,128)S(1)} %slice.34) | copy-start | bytes 1572868
  125.9 38.4 %copy-start.3 = (bf16[32,8,128]{2,1,0:T(8,128)(2,1)S(1)}, bf16[32,8,128]{2,1,0:T(8,128)(2,1)}, u32[]{:S(2)}) copy-start(bf16[32,8,128]{2,1,0:T(8,128)(2,1)} %all-reduce.3.cloned.1.call-done) | copy-start | bytes 196612
  165.1 216.0 %all-gather.2.cloned.1.call-start = ((), (), s32[]{:S(2)}) async-start(), calls=%async_computation.2 | async-start | bytes 8650752 | tf_op jit(solution)/shard_map/all_gather | solution.py:52
  165.6 824.3 %reduce-scatter.5.cloned.1.call-start = ((), (), s32[]{:S(2)}) async-start(), calls=%async_computation.6 | async-start | bytes 73728 | tf_op jit(solution)/shard_map/reduce_scatter | solution.py:141
  551.6 5.6 copy-start.4
  558.9 468.6 %reduce-scatter.3.cloned.1.call-start = ((), (), s32[]{:S(2)}) async-start(), calls=%async_computation.5 | async-start | bytes 2359296 | tf_op jit(solution)/shard_map/reduce_scatter | solution.py:138
  558.9 470.5 %copy-start.1 = (bf16[512,128]{1,0:T(8,128)(2,1)S(1)}, bf16[512,128]{1,0:T(8,128)(2,1)}, u32[]{:S(2)}) copy-start(bf16[512,128]{1,0:T(8,128)(2,1)} %param.12) | copy-start | bytes 393220
  562.6 464.9 %copy-start.6 = (f32[256]{0:T(256)S(1)}, f32[256]{0:T(256)}, u32[]{:S(2)}) copy-start(f32[256]{0:T(256)} %param.16) | copy-start | bytes 3076
Sparse Core Ops, SparseCore 0:
  63.3 61.7 all-reduce.2
  165.2 175.8 all-reduce.4
  559.0 430.9 reduce-scatter.4
  992.5 34.9 reduce-scatter.2
Sparse Core Ops, SparseCore 1:
  168.0 213.0 all-gather.1
where the time goes:
time: 1040 us
  waiting for transfers between devices  736 us (71%)
  local copies, waits for them, and re-layouts  99.6 us (10%)
  other arithmetic  96.5 us (9%)
  blocking collectives  52.3 us (5%)
  matrix products  35 us (3%)
  between operations  15.4 us (1%)
    reduce_scatter x1, waiting for transfers between devices, on_device(): lax.psum_scatter(denominator_rows.astype(jnp.bfloat16), 'src', scatter_di...  424 us
    pmax x1, waiting for transfers between devices, on_device(): maxima = lax.pmax(maxima.astype(jnp.bfloat16), 'src').astype(maxima.dtype)  175 us
    psum x1, waiting for transfers between devices, from_root(): return lax.psum(block, axis)  61 us
    all_gather x1, blocking collectives, on_device(): lax.all_gather(terms_of(projected, source_att, target_att).astype(jnp.bfl...  52.3 us
    all_gather x1, waiting for transfers between devices, on_device(): lax.all_gather(projected.astype(jnp.bfloat16), 'dst', axis=0, tiled=True)  38.5 us
    reduce_scatter x1, waiting for transfers between devices, on_device(): lax.psum_scatter(weighted_rows.astype(jnp.bfloat16), 'src', scatter_dimen...  36.6 us
    dot_general x4, matrix products, sum_step(): jnp.einsum('ghab,gbhc->gahc', rounded, value_blocks[col_ids], preferred_e...  33.1 us
    reduce_sum x4, other arithmetic, sum_step(): denominator = denominator.at[row_ids].add(jnp.sum(weight, axis=3))  30.6 us
  transfers between devices with their start and end apart: 5, of which 5 were waited for; matrix products, arithmetic and copies ran while one was open for 1% of the time, Pallas kernels for 0%

commit v1 on v0

--- a/solution.py
+++ b/solution.py
@@ -6,6 +6,12 @@
 
 HEADS = 8
 HEAD_DIM = 32
+
+
+def scan_meshes_up(sheet, array_axis=0):
+    return jnp.concatenate(
+        lax.all_to_all(jnp.stack([sheet] * lax.psum(1, "dst")), "dst", 0, 0), array_axis
+    )
 
 
 def from_root(block, axis, holder):
@@ -49,7 +55,7 @@
     feature_width = projection.shape[1]
     projected = jnp.dot(features, projection, preferred_element_type=jnp.float32)
     gathered, score_terms = (
-        lax.all_gather(projected.astype(jnp.bfloat16), "dst", axis=0, tiled=True),
+        scan_meshes_up(projected.astype(jnp.bfloat16)),
         lax.all_gather(
             terms_of(projected, source_att, target_att).astype(jnp.bfloat16),
             "dst",

time: 1040 us -> 1200 us (1.15)
  blocking collectives: 52.3 us -> 238 us
  waiting for transfers between devices: 736 us -> 678 us
  local copies, waits for them, and re-layouts: 99.6 us -> 120 us
    all_gather x1, blocking collectives: 52.3 us -> 238 us  [on_device(): lax.all_gather(terms_of(projected, source_att, target_att).astype(jnp.bfl...]
    all_gather x1 -> x0, waiting for transfers between devices: 38.5 us -> none  [on_device(): lax.all_gather(projected.astype(jnp.bfloat16), 'dst', axis=0, tiled=True)]
    while x2 -> x3, local copies, waits for them, and re-layouts: 30 us -> 53.5 us  [on_device(): weighted, denominator = lax.fori_loop(0, steps_live, sum_step, start_state)]
    reduce_scatter x1, waiting for transfers between devices: 424 us -> 407 us  [on_device(): lax.psum_scatter(denominator_rows.astype(jnp.bfloat16), 'src', scatter_di...]
  transfers between devices with their start and end apart: 5 -> 5, of which waited for: 5 -> 4; matrix products, arithmetic and copies ran while one was open for 1% -> 5% of each run, Pallas kernels for 0% -> 0%
where the time goes in v1:
time: 1200 us; the launch traced here: 1190 us
  waiting for transfers between devices  678 us (56%)
  blocking collectives  238 us (20%)
  local copies, waits for them, and re-layouts  120 us (10%)
  other arithmetic  96.8 us (8%)
  matrix products  34.3 us (3%)
  between operations  14 us (1%)
    reduce_scatter x1, waiting for transfers between devices, on_device(): lax.psum_scatter(denominator_rows.astype(jnp.bfloat16), 'src', scatter_di...  407 us
    all_gather x1, blocking collectives, on_device(): lax.all_gather(terms_of(projected, source_att, target_att).astype(jnp.bfl...  238 us
    pmax x1, waiting for transfers between devices, on_device(): maxima = lax.pmax(maxima.astype(jnp.bfloat16), 'src').astype(maxima.dtype)  175 us
    psum x1, waiting for transfers between devices, from_root(): return lax.psum(block, axis)  59.5 us
    while x3, local copies, waits for them, and re-layouts, on_device(): weighted, denominator = lax.fori_loop(0, steps_live, sum_step, start_state)  53.5 us
    reduce_scatter x1, waiting for transfers between devices, on_device(): lax.psum_scatter(weighted_rows.astype(jnp.bfloat16), 'src', scatter_dimen...  36.6 us
    dot_general x4, matrix products, sum_step(): jnp.einsum('ghab,gbhc->gahc', rounded, value_blocks[col_ids], preferred_e...  33.1 us
    reduce_sum x4, other arithmetic, sum_step(): denominator = denominator.at[row_ids].add(jnp.sum(weight, axis=3))  30.6 us
  transfers between devices with their start and end apart: 5, of which 4 were waited for; matrix products, arithmetic and copies ran while one was open for 5% of the time, Pallas kernels for 0%

profile of v1, /device:TPU:8, one launch (start us, length us, event | category | flops | bytes accessed | tf_op | source)
XLA Modules:
  0.0 1192.9 jit_solution(16041884827673842212)
XLA Ops:
  7.4 1.2 bitcast_reduce_fusion.1
  8.7 4.2 stack.2
  12.8 11.8 all-to-all-start
  24.7 237.8 %all_gather.3 = bf16[16,16384]{1,0:T(8,128)(2,1)S(1)} all-gather(bf16[16,512]{1,0:T(8,128)(2,1)S(1)} %maximum_bitcast_fusion), channel_id=1, replica_groups=mesh['dst'=32,'src'=8] {'dst'}, dimensions={1}, use_global_device_ids=true | all-gather | bytes 540672 | tf_op jit(solution)/shard_map/all_gather | solution.py:59
  264.1 59.5 %all-reduce.3.cloned.1.call-done = bf16[32,8,128]{2,1,0:T(8,128)(2,1)} async-done(((bf16[32,8,128]{2,1,0:T(8,128)(2,1)}), bf16[32,8,128]{2,1,0:T(8,128)(2,1)}) %all-reduce.3.cloned.1.call-update) | async-done | bytes 65552 | tf_op jit(solution)/shard_map/psum | solution.py:19
  324.5 38.4 %while.22 = (s32[]{:T(128)}, f32[32,8,128]{2,1,0:T(8,128)S(1)}, s32[]{:T(128)}, s32[2,256]{1,0:T(2,128)S(1)}, s32[256,16,128]{2,1,0:T(8,128)}, /*index=5*/s32[]{...) while((s32[]{:T(128)}, f32[32,8,128]{2,1,0:T(8,128)S(1)}, ...), condition=%wide.region_6.7_spmd, body=%wide.region_3.6_spmd.sunk | while | flops 13633670 | bytes 2112275 | solution.py:107
  328.2 4.7 fusion.61
  337.8 4.7 fusion.61
  347.4 4.7 fusion.61
  352.1 1.1 scatter_fusion
  357.0 4.7 fusion.61
  361.7 1.1 scatter_fusion
  363.6 174.9 %all-reduce.5.cloned.1.call-done = bf16[32,8,128]{2,1,0:T(8,128)(2,1)} async-done(((bf16[32,8,128]{2,1,0:T(8,128)(2,1)}), bf16[32,8,128]{2,1,0:T(8,128)(2,1)}) %all-reduce.5.cloned.1.call-update) | async-done | bytes 65552 | tf_op jit(solution)/shard_map/pmax | solution.py:111
  539.4 11.9 %copy.66 = bf16[32,512,256]{2,1,0:T(8,128)(2,1)} copy(bf16[32,512,256]{1,2,0:T(8,128)(2,1)} %all-to-all-done) | data formatting | bytes 16777216 | tf_op jit(solution)/shard_map/while | solution.py:130
  551.3 36.0 %reshape.262 = bf16[128,128,8,32]{3,2,1,0:T(8,128)(2,1)} reshape(bf16[32,512,256]{2,1,0:T(8,128)(2,1)} %copy.66) | data formatting | bytes 16777216 | tf_op jit(solution)/shard_map/while | solution.py:130
  587.3 1.7 constant_dynamic-slice_fusion.6
  589.0 3.4 copy.62
  592.4 2.4 broadcast_in_dim.36
  594.9 130.8 %while.23 = (s32[]{:T(128)}, f32[32,128,256]{2,1,0:T(8,128)}, f32[32,8,128]{2,1,0:T(8,128)S(1)}, s32[]{:T(128)}, s32[2,256]{1,0:T(2,128)S(1)}, /*index=5*/bf16[1...) while((s32[]{:T(128)}, f32[32,128,256]{2,1,0:T(8,128)}, ...), condition=%wide.region_12.13_spmd, body=%wide.region_8.12_spmd.sunk | while | flops 165152896 | bytes 18496492 | solution.py:130
  599.2 7.7 fusion.68
  606.9 1.1 scatter_fusion.2
  608.0 4.9 gather_fusion.2
  612.8 8.3 fusion.67
  621.1 1.9 copy.77
  623.0 4.5 scatter_fusion.1
  631.9 7.7 fusion.68
  640.6 5.0 gather_fusion.2
  645.6 8.3 fusion.67
  653.9 1.9 copy.77
  655.8 4.5 scatter_fusion.1
  664.6 7.7 fusion.68
  672.3 1.1 scatter_fusion.2
  673.4 4.9 gather_fusion.2
  678.3 8.3 fusion.67
  686.5 1.9 copy.77
  688.5 4.4 scatter_fusion.1
  697.2 7.7 fusion.68
  706.0 4.9 gather_fusion.2
  710.8 8.3 fusion.67
  719.1 1.9 copy.77
  721.0 4.6 scatter_fusion.1
  725.6 1.6 fusion.42
  727.3 5.6 copy.63
  732.9 4.5 fusion.35
  737.4 2.9 copy.64
  740.3 406.5 %reduce-scatter.5.cloned.1.call-done = bf16[8,512]{1,0:T(8,128)(2,1)} async-done(((bf16[8,4096]{1,0:T(8,128)(2,1)}), bf16[8,512]{1,0:T(8,128)(2,1)}) %reduce-scatter.5.cloned.1.call-update) | async-done | bytes 8208 | tf_op jit(solution)/shard_map/reduce_scatter | solution.py:147
  1147.8 36.6 %reduce-scatter.3.cloned.1.call-done = bf16[512,256]{1,0:T(8,128)(2,1)} async-done(((bf16[4096,256]{1,0:T(8,128)(2,1)}), bf16[512,256]{1,0:T(8,128)(2,1)}) %reduce-scatter.3.cloned.1.call-update) | async-done | bytes 262160 | tf_op jit(solution)/shard_map/reduce_scatter | solution.py:144
  1184.4 1.9 fusion.37
  (142 shorter events, 41.3 us)
Async XLA Ops:
  6.5 0.9 copy-start
  12.8 526.5 %all-to-all-start = ((bf16[32,512,256]{1,2,0:T(8,128)(2,1)}), bf16[32,512,256]{1,2,0:T(8,128)(2,1)}, u32[]{:S(2)}, u32[]{:S(2)}) async-start(bf16[32,512,256]{1,2,0:T(8,128)(2,1)} %stack.2), calls=%async_computation | async-start | bytes 16777216 | tf_op jit(solution)/shard_map/all_to_all | solution.py:13
  24.6 299.9 %copy-start.5 = (s32[1,1,2,256]{3,2,1,0:T(2,128)S(1)}, s32[1,1,2,256]{3,2,1,0:T(2,128)}, u32[]{:S(2)}) copy-start(s32[1,1,2,256]{3,2,1,0:T(2,128)} %param.17) | copy-start | bytes 6148
  24.6 299.0 %all-reduce.3.cloned.1.call-start = ((), (), s32[]{:S(2)}) async-start(), calls=%async_computation.3 | async-start | bytes 131072 | tf_op jit(solution)/shard_map/psum | solution.py:19
  263.2 275.3 %all-reduce.5.cloned.1.call-start = ((), (), s32[]{:S(2)}) async-start(), calls=%async_computation.4 | async-start | bytes 131072 | tf_op jit(solution)/shard_map/pmax | solution.py:111
  264.0 98.8 %copy-start.2 = (f32[8,16384]{1,0:T(8,128)}, f32[8,16384]{1,0:T(8,128)S(1)}, u32[]{:S(2)}) copy-start(f32[8,16384]{1,0:T(8,128)S(1)} %slice.34) | copy-start | bytes 1572868
  324.4 38.4 %copy-start.3 = (bf16[32,8,128]{2,1,0:T(8,128)(2,1)S(1)}, bf16[32,8,128]{2,1,0:T(8,128)(2,1)}, u32[]{:S(2)}) copy-start(bf16[32,8,128]{2,1,0:T(8,128)(2,1)} %all-reduce.3.cloned.1.call-done) | copy-start | bytes 196612
  363.5 783.3 %reduce-scatter.5.cloned.1.call-start = ((), (), s32[]{:S(2)}) async-start(), calls=%async_computation.6 | async-start | bytes 73728 | tf_op jit(solution)/shard_map/reduce_scatter | solution.py:147
  594.9 130.8 %copy-start.4 = (bf16[32,8,128]{2,1,0:T(8,128)(2,1)S(1)}, bf16[32,8,128]{2,1,0:T(8,128)(2,1)}, u32[]{:S(2)}) copy-start(bf16[32,8,128]{2,1,0:T(8,128)(2,1)} %all-reduce.5.cloned.1.call-done) | copy-start | bytes 196612
  727.3 457.1 %reduce-scatter.3.cloned.1.call-start = ((), (), s32[]{:S(2)}) async-start(), calls=%async_computation.5 | async-start | bytes 2359296 | tf_op jit(solution)/shard_map/reduce_scatter | solution.py:144
  732.9 453.4 %copy-start.1 = (bf16[512,128]{1,0:T(8,128)(2,1)S(1)}, bf16[512,128]{1,0:T(8,128)(2,1)}, u32[]{:S(2)}) copy-start(bf16[512,128]{1,0:T(8,128)(2,1)} %param.12) | copy-start | bytes 393220
  737.4 447.0 %copy-start.6 = (f32[256]{0:T(256)S(1)}, f32[256]{0:T(256)}, u32[]{:S(2)}) copy-start(f32[256]{0:T(256)} %param.16) | copy-start | bytes 3076
Sparse Core Ops, SparseCore 0:
  263.3 60.2 all-reduce.2
  363.7 174.7 all-reduce.4
  727.4 419.4 reduce-scatter.4
  1149.4 34.9 reduce-scatter.2
